TPU v7x, 512 devices: a whole 4x4x16 slice. The times are simulated.
512 devices in a mesh: mp: 64 (over x, z), replica: 8 (over y, core).
Axes of the slice: x: 4, y: 4, z: 16, core: 2. Of those that a mesh axis runs over, the one named last changes fastest.
Arguments:
- pooled_grads: bfloat16 [64, 8, 128, 64, 128], P('mp', 'replica'), may hold values from -0.119628906 to 0.119628906
- table: float32 [64, 512, 128], P('mp'), may hold values from -3 to 3
- state: float32 [64, 512], P('mp'), may hold values from 0.2 to 5
- tile_mult: bfloat16 [64, 8, 64, 128, 128], P('mp', 'replica'), may hold values from 0 to 3, as said below
- tile_rows: int32 [64, 8, 64], P('mp', 'replica'), may hold values from 0 to 3
Outputs:
- new_table: float32 [64, 512, 128], P('mp')
- new_state: float32 [64, 512], P('mp')
Inputs may be any that keep to these rules, and one draw needn't show every extreme that they name: tile_mult holds whole numbers.
All inputs are finite; a program needn't handle non-finite values.
Results may differ from a plain program's by a relative error of at most 0.0003.
Values may be sent and summed in bfloat16 or wider, within the bound.
No kernel may reach another device: no remote copies, remote signals or barrier semaphores. Data moves between devices by JAX's collectives and lax.ppermute only.
A program may use at most 64 MiB of HBM per device.

v0:
```python
import jax
import jax.numpy as jnp
from jax import lax
from jax.sharding import PartitionSpec as P

LEARN_RATE = 0.5
EPSILON = 1e-06


def adagrad(weights_in, accum_in, gradient):
    accum_out = accum_in + jnp.mean(gradient * gradient, axis=-1)
    weights_out = weights_in - LEARN_RATE * gradient / (jnp.sqrt(accum_out)[..., None] + EPSILON)
    return (weights_out, accum_out)


def on_device(pooled_grads, table, state, tile_mult, tile_rows):
    local_grads = pooled_grads[0, 0]
    width = local_grads.shape[-1]
    received = lax.all_to_all(local_grads, "mp", split_axis=1, concat_axis=0, tiled=True)
    counts_bf = tile_mult[0, 0]
    block_size = counts_bf.shape[-1]
    sample_blocks = received.reshape(-1, block_size, width)
    row_ids = tile_rows[0, 0]
    contrib = jnp.einsum(
        "tsr,tse->tre", counts_bf, sample_blocks, preferred_element_type=jnp.float32
    )
    weights_in = table[0]
    accum_in = state[0]
    row_count = weights_in.shape[0]
    row_blocks = row_count // block_size
    onehot = (row_ids[:, None] == jnp.arange(row_blocks, dtype=jnp.int32)[None, :]).astype(
        jnp.float32
    )
    partial_grad = jnp.einsum(
        "tb,tre->bre", onehot, contrib, precision=lax.Precision.HIGHEST
    ).reshape(row_count, width)
    total_grad = lax.psum(partial_grad, "replica")
    weights_out, accum_out = adagrad(weights_in, accum_in, total_grad)
    return (weights_out[None], accum_out[None])


def solution(mesh):
    placed = (
        P("mp", "replica", None, None, None),
        P("mp", None, None),
        P("mp", None),
        P("mp", "replica", None, None, None),
        P("mp", "replica", None),
    )
    return jax.shard_map(
        on_device,
        mesh=mesh,
        in_specs=placed,
        out_specs=(P("mp", None, None), P("mp", None)),
        check_vma=False,
    )
```

profile of v0, /device:TPU:2, one launch (start us, length us, event | category | flops | bytes accessed | tf_op | source)
XLA Modules:
  0.0 211.9 jit_solution(7404038184944069721)
XLA Ops:
  7.2 0.0 copy-start
  7.2 0.0 all-reduce.2.cloned.1.call-start
  7.2 3.1 %copy.16 = bf16[1,1,128,64,128]{4,2,3,1,0:T(8,128)(2,1)S(1)} copy(bf16[1,1,128,64,128]{4,3,2,1,0:T(8,128)(2,1)} %param.5) | data formatting | bytes 4194304 | tf_op args[0]
  10.3 115.6 %all_to_all.15 = bf16[128,64,128]{2,0,1:T(8,128)(2,1)S(1)} all-to-all(bf16[128,64,128]{2,0,1:T(8,128)(2,1)S(1)} %bitcast.26), channel_id=1, replica_groups=mesh['mp'=64,'replica'=8] {'mp'}, dimensions={1} | all-to-all | bytes 4194304 | tf_op jit(solution)/shard_map/all_to_all | solution.py:19
  125.9 0.0 copy-done
  125.9 0.0 copy-start.3
  126.0 0.9 fusion.2
  126.8 0.0 copy-done.3
  126.8 0.0 copy-start.2
  126.9 0.0 copy-start.1
  126.9 3.8 %fusion = f32[4,128,128]{2,0,1:T(4,128)S(1)} fusion(f32[64,128,128]{2,1,0:T(8,128)S(1)} %fusion.2, s32[64]{0:T(128)S(1)} %bitcast.30), kind=kOutput, calls=%fused_computation | convolution fusion | flops 50331904 | bytes 4456704 | tf_op jit(solution)/shard_map/tb,tre->bre/dot_general | solution.py:34
  130.7 0.7 copy.11
  131.4 0.0 all-reduce.2.cloned.1.call-update
  131.4 70.1 %all-reduce.2.cloned.1.call-done = f32[512,128]{1,0:T(8,128)} async-done(((f32[512,128]{1,0:T(8,128)}), f32[512,128]{1,0:T(8,128)}) %all-reduce.2.cloned.1.call-update) | async-done | bytes 262160 | tf_op jit(solution)/shard_map/psum | solution.py:37
  201.5 1.1 multiply_reduce_fusion
  202.6 0.0 copy-done.2
  202.6 0.6 add.26
  203.2 0.0 copy-done.1
  203.2 1.8 fusion.5
  (1 shorter events, 0.0 us)
Async XLA Ops:
  7.2 118.8 %copy-start = (bf16[1,1,64,128,128]{4,3,2,1,0:T(8,128)(2,1)S(1)}, bf16[1,1,64,128,128]{4,3,2,1,0:T(8,128)(2,1)}, u32[]{:S(2)}) copy-start(bf16[1,1,64,128,128]{4,3,2,1,0:T(8,128)(2,1)} %param.8) | copy-start | bytes 6291460
  7.2 194.3 %all-reduce.2.cloned.1.call-start = ((), (), s32[]{:S(2)}) async-start(), calls=%async_computation.1 | async-start | bytes 524288 | tf_op jit(solution)/shard_map/psum | solution.py:37
  125.9 0.9 copy-start.3
  126.8 75.8 %copy-start.2 = (f32[1,512]{1,0:T(1,128)S(1)}, f32[1,512]{1,0:T(1,128)}, u32[]{:S(2)}) copy-start(f32[1,512]{1,0:T(1,128)} %param.7) | copy-start | bytes 6148
  126.9 76.4 %copy-start.1 = (f32[1,512,128]{2,1,0:T(8,128)S(1)}, f32[1,512,128]{2,1,0:T(8,128)}, u32[]{:S(2)}) copy-start(f32[1,512,128]{2,1,0:T(8,128)} %param.6) | copy-start | bytes 786436
Sparse Core Ops, SparseCore 0:
  131.5 69.9 all-reduce.1
where the time goes:
time: 212 us
  blocking collectives  116 us (55%)
  waiting for transfers between devices  70.1 us (33%)
  between operations  14.1 us (7%)
  matrix products  4.67 us (2%)
  local copies, waits for them, and re-layouts  3.83 us (2%)
  other arithmetic  3.48 us (2%)
    all_to_all x1, blocking collectives, on_device(): lax.all_to_all(local_grads, 'mp', split_axis=1, concat_axis=0, tiled=True)  116 us
    psum x1, waiting for transfers between devices, on_device(): total_grad = lax.psum(partial_grad, 'replica')  70.1 us
  transfers between devices with their start and end apart: 1, of which 1 were waited for; matrix products, arithmetic and copies ran while one was open for 0% of the time, Pallas kernels for 0%

commit v1 on v0

--- a/solution.py
+++ b/solution.py
@@ -34,7 +34,11 @@
     partial_grad = jnp.einsum(
         "tb,tre->bre", onehot, contrib, precision=lax.Precision.HIGHEST
     ).reshape(row_count, width)
-    total_grad = lax.psum(partial_grad, "replica")
+    total_grad = partial_grad
+    for hop in (1, 2, 4):
+        total_grad = total_grad + lax.ppermute(
+            total_grad, "replica", [(dev, dev ^ hop) for dev in range(8)]
+        )
     weights_out, accum_out = adagrad(weights_in, accum_in, total_grad)
     return (weights_out[None], accum_out[None])
 

time: 212 us -> 151 us (0.71)
  the two profiles are of different devices: /device:TPU:2 before, /device:TPU:38 now
where the time goes in v1:
time: 151 us
  blocking collectives  116 us (77%)
  waiting for transfers between devices  14 us (9%)
  starting transfers between devices  10.6 us (7%)
  matrix products  4.67 us (3%)
  local copies, waits for them, and re-layouts  3.13 us (2%)
  other arithmetic  1.64 us (1%)
    all_to_all x1, blocking collectives, on_device(): lax.all_to_all(local_grads, 'mp', split_axis=1, concat_axis=0, tiled=True)  116 us
    ppermute x3, waiting for transfers between devices, on_device(): lax.ppermute(total_grad, 'replica', [(dev, dev ^ hop) for dev in range(8)])  14 us
    ppermute x3, starting transfers between devices, on_device(): lax.ppermute(total_grad, 'replica', [(dev, dev ^ hop) for dev in range(8)])  10.6 us
    dot_general x1, matrix products, on_device(): jnp.einsum('tb,tre->bre', onehot, contrib, precision=lax.Precision.HIGHEST)  3.8 us
    unnamed x9, local copies, waits for them, and re-layouts  3.12 us
  transfers between devices with their start and end apart: 3, of which 3 were waited for; matrix products, arithmetic and copies ran while one was open for 0% of the time, Pallas kernels for 0%

profile of v1, /device:TPU:38, one launch (start us, length us, event | category | flops | bytes accessed | tf_op | source)
XLA Modules:
  0.0 151.1 jit_solution(3645059440562759108)
XLA Ops:
  0.6 0.0 copy-start
  0.6 3.1 %copy.16 = bf16[1,1,128,64,128]{4,2,3,1,0:T(8,128)(2,1)S(1)} copy(bf16[1,1,128,64,128]{4,3,2,1,0:T(8,128)(2,1)} %param.5) | data formatting | bytes 4194304 | tf_op args[0]
  3.7 116.3 %all_to_all.15 = bf16[128,64,128]{2,0,1:T(8,128)(2,1)S(1)} all-to-all(bf16[128,64,128]{2,0,1:T(8,128)(2,1)S(1)} %bitcast.27), channel_id=1, replica_groups=mesh['mp'=64,'replica'=8] {'mp'}, dimensions={1} | all-to-all | bytes 4194304 | tf_op jit(solution)/shard_map/all_to_all | solution.py:19
  120.0 0.0 copy-done
  120.0 0.0 copy-start.3
  120.0 0.9 fusion.2
  120.9 0.0 copy-done.3
  120.9 3.8 %fusion = f32[4,128,128]{2,0,1:T(4,128)S(1)} fusion(f32[64,128,128]{2,1,0:T(8,128)S(1)} %fusion.2, s32[64]{0:T(128)S(1)} %bitcast.31), kind=kOutput, calls=%fused_computation | convolution fusion | flops 50331904 | bytes 4456704 | tf_op jit(solution)/shard_map/tb,tre->bre/dot_general | solution.py:34
  124.7 0.0 copy-start.2
  124.7 0.0 copy-start.1
  124.8 2.1 %collective-permute-start = (f32[512,128]{1,0:T(8,128)S(1)}, f32[512,128]{1,0:T(8,128)S(1)}, u32[]{:S(2)}, u32[]{:S(2)}) collective-permute-start(f32[512,128]{1,0:T(8,128)S(1)} %bitcast.28), channel_id=1, source_target_pairs={{0,1},{1,0},{2,3},{3,2},{4,5},{5,4},{6,7},{7,6},{8,9},{9,8},{10,11... | collective-permute-start | bytes 786440 | tf_op jit(solution)/shard_map/ppermute | solution.py:39
  126.8 1.5 collective-permute-done
  128.3 3.5 %collective-permute-start.1 = (f32[512,128]{1,0:T(8,128)S(1)}, f32[512,128]{1,0:T(8,128)S(1)}, u32[]{:S(2)}, u32[]{:S(2)}) collective-permute-start(f32[512,128]{1,0:T(8,128)S(1)} %bitcast_add_fusion), channel_id=1, source_target_pairs={{0,2},{1,3},{2,0},{3,1},{4,6},{5,7},{6,4},{7,5},{8,10},{9,11},{10,... | collective-permute-start | bytes 786440 | tf_op jit(solution)/shard_map/ppermute | solution.py:39
  131.8 6.7 %collective-permute-done.1 = f32[512,128]{1,0:T(8,128)S(1)} collective-permute-done((f32[512,128]{1,0:T(8,128)S(1)}, f32[512,128]{1,0:T(8,128)S(1)}, u32[]{:S(2)}, u32[]{:S(2)}) %collective-permute-start.1) | collective-permute-done | bytes 262176 | tf_op jit(solution)/shard_map/ppermute | solution.py:39
  138.6 5.1 %collective-permute-start.2 = (f32[512,128]{1,0:T(8,128)S(1)}, f32[512,128]{1,0:T(8,128)S(1)}, u32[]{:S(2)}, u32[]{:S(2)}) collective-permute-start(f32[512,128]{1,0:T(8,128)S(1)} %add.31), channel_id=1, source_target_pairs={{0,4},{1,5},{2,6},{3,7},{4,0},{5,1},{6,2},{7,3},{8,12},{9,13},{10,... | collective-permute-start | bytes 786440 | tf_op jit(solution)/shard_map/ppermute | solution.py:39
  143.7 5.8 %collective-permute-done.2 = f32[512,128]{1,0:T(8,128)S(1)} collective-permute-done((f32[512,128]{1,0:T(8,128)S(1)}, f32[512,128]{1,0:T(8,128)S(1)}, u32[]{:S(2)}, u32[]{:S(2)}) %collective-permute-start.2) | collective-permute-done | bytes 262176 | tf_op jit(solution)/shard_map/ppermute | solution.py:39
  149.5 0.1 multiply_reduce_fusion
  149.7 0.0 copy-done.2
  149.7 0.6 add.36
  150.3 0.0 copy-done.1
  150.3 0.8 fusion.5
  (4 shorter events, 0.1 us)
Async XLA Ops:
  0.6 119.4 %copy-start = (bf16[1,1,64,128,128]{4,3,2,1,0:T(8,128)(2,1)S(1)}, bf16[1,1,64,128,128]{4,3,2,1,0:T(8,128)(2,1)}, u32[]{:S(2)}) copy-start(bf16[1,1,64,128,128]{4,3,2,1,0:T(8,128)(2,1)} %param.8) | copy-start | bytes 6291460
  120.0 0.9 copy-start.3
  124.7 25.0 %copy-start.2 = (f32[1,512]{1,0:T(1,128)S(1)}, f32[1,512]{1,0:T(1,128)}, u32[]{:S(2)}) copy-start(f32[1,512]{1,0:T(1,128)} %param.7) | copy-start | bytes 6148
  124.7 25.6 %copy-start.1 = (f32[1,512,128]{2,1,0:T(8,128)S(1)}, f32[1,512,128]{2,1,0:T(8,128)}, u32[]{:S(2)}) copy-start(f32[1,512,128]{2,1,0:T(8,128)} %param.6) | copy-start | bytes 786436
  124.8 3.6 %collective-permute-start = (f32[512,128]{1,0:T(8,128)S(1)}, f32[512,128]{1,0:T(8,128)S(1)}, u32[]{:S(2)}, u32[]{:S(2)}) collective-permute-start(f32[512,128]{1,0:T(8,128)S(1)} %bitcast.28), channel_id=1, source_target_pairs={{0,1},{1,0},{2,3},{3,2},{4,5},{5,4},{6,7},{7,6},{8,9},{9,8},{10,11... | collective-permute-start | bytes 786440 | tf_op jit(solution)/shard_map/ppermute | solution.py:39
  128.3 10.2 %collective-permute-start.1 = (f32[512,128]{1,0:T(8,128)S(1)}, f32[512,128]{1,0:T(8,128)S(1)}, u32[]{:S(2)}, u32[]{:S(2)}) collective-permute-start(f32[512,128]{1,0:T(8,128)S(1)} %bitcast_add_fusion), channel_id=1, source_target_pairs={{0,2},{1,3},{2,0},{3,1},{4,6},{5,7},{6,4},{7,5},{8,10},{9,11},{10,... | collective-permute-start | bytes 786440 | tf_op jit(solution)/shard_map/ppermute | solution.py:39
  138.6 10.9 %collective-permute-start.2 = (f32[512,128]{1,0:T(8,128)S(1)}, f32[512,128]{1,0:T(8,128)S(1)}, u32[]{:S(2)}, u32[]{:S(2)}) collective-permute-start(f32[512,128]{1,0:T(8,128)S(1)} %add.31), channel_id=1, source_target_pairs={{0,4},{1,5},{2,6},{3,7},{4,0},{5,1},{6,2},{7,3},{8,12},{9,13},{10,... | collective-permute-start | bytes 786440 | tf_op jit(solution)/shard_map/ppermute | solution.py:39
